TPU v7x, 512 devices: a whole 4x8x8 slice. The times are simulated.
512 devices in a mesh: grid: 16 (over y, core), dom: 32 (over z, x).
Axes of the slice: x: 4, y: 8, z: 8, core: 2. Of those that a mesh axis runs over, the one named last changes fastest.
Arguments:
- state: float32 [5, 125, 65536], P(None, None, ('grid', 'dom')), as said below
- inv_size: float32 [3, 65536], P(None, ('grid', 'dom')), may hold values from 1 to 4
- plus_order: int32 [3, 65536], P(None, ('grid', 'dom')), may hold values from 0 to 127, as said below
- minus_order: int32 [3, 65536], P(None, ('grid', 'dom')), may hold values from 0 to 127, as said below
- donor_cell: int32 [512, 1024], P(('grid', 'dom')), may hold values from 0 to 127
- donor_weights: float32 [512, 3, 5, 1024], P(('grid', 'dom')), as said below
- recv_slot: int32 [512, 600], P(('grid', 'dom')), may hold values from 0 to 1023, as said below
Outputs:
- rhs: float32 [5, 125, 65536], P(None, None, ('grid', 'dom'))
Inputs may be any that keep to these rules, and one draw needn't show every extreme that they name: `plus_order`: within each device's block of 128 columns, every row is a permutation of the local element numbers. `minus_order`: within each device's block of 128 columns, every row is a permutation of the local element numbers. `state`: density lies in [0.9, 1.1], each momentum in [-0.1, 0.1], energy in [2.4, 2.6]. `donor_weights`: for each donor device, direction and slot, the five weights are the Lagrange basis of the five Gauss-Legendre points evaluated at one coordinate in [-0.8, 0.8]. `recv_slot`: entries of one device's row are distinct, and each names a slot whose source device (the slot // 2) lies in another grid than the row's device.
All inputs are finite; a program needn't handle non-finite values.
Results may differ from a plain program's by a relative error of at most 0.0003.
Values sent between devices are 32-bit elements; how exact they have to be, the bound alone decides.
A program may use at most 64 MiB of HBM per device.

v0:
```python
import math
import jax
import jax.numpy as jnp
from jax import lax
from jax.sharding import PartitionSpec as P

precise = lax.Precision.HIGHEST
volume_forms = ("ia,vabce->vibce", "ib,vabce->vaice", "ic,vabce->vabie")
face_forms = ("a,vabce->vbce", "b,vabce->vace", "c,vabce->vabe")
lift_forms = ("i,vbce->vibce", "i,vace->vaice", "i,vabe->vabie")


def gauss_nodes():
    outer = math.sqrt(5.0 + 2.0 * math.sqrt(10.0 / 7.0)) / 3.0
    inner = math.sqrt(5.0 - 2.0 * math.sqrt(10.0 / 7.0)) / 3.0
    return [-outer, -inner, 0.0, inner, outer]


def basis_value(nodes, column, target_positions):
    value = 1.0
    for other in range(5):
        if other != column:
            value = value * (target_positions - nodes[other]) / (nodes[column] - nodes[other])
    return value


def basis_slope(nodes, column, target_positions):
    total = 0.0
    for skipped in range(5):
        if skipped != column:
            value = 1.0 / (nodes[column] - nodes[skipped])
            for other in range(5):
                if other != column and other != skipped:
                    value = (
                        value * (target_positions - nodes[other]) / (nodes[column] - nodes[other])
                    )
            total = total + value
    return total


def legendre_slopes(target_positions):
    values = [1.0, target_positions]
    slopes = [0.0, 1.0]
    for order in range(1, 5):
        values.append(
            ((2 * order + 1) * target_positions * values[order] - order * values[order - 1])
            / (order + 1)
        )
        slopes.append(slopes[order - 1] + (2 * order + 1) * values[order])
    return (slopes[4], slopes[5])


def tables():
    nodes = gauss_nodes()
    deriv = [[basis_slope(nodes, column, nodes[row]) for column in range(5)] for row in range(5)]
    lower = [basis_value(nodes, column, -1.0) for column in range(5)]
    upper = [basis_value(nodes, column, 1.0) for column in range(5)]
    lift_low = []
    lift_high = []
    for row in range(5):
        slope_four, slope_five = legendre_slopes(nodes[row])
        lift_low.append(-0.5 * (slope_five - slope_four))
        lift_high.append(0.5 * (slope_five + slope_four))
    return tuple(
        (jnp.asarray(matrix, jnp.float32) for matrix in (deriv, lower, upper, lift_low, lift_high))
    )


def euler_flux(state, direction):
    density = state[0]
    momenta = state[1:4]
    energy = state[4]
    speed = momenta[direction] / density
    pressure = 0.4 * (energy - 0.5 * jnp.sum(momenta * momenta, axis=0) / density)
    pieces = [
        momenta[direction],
        momenta[0] * speed,
        momenta[1] * speed,
        momenta[2] * speed,
        (energy + pressure) * speed,
    ]
    pieces[1 + direction] = pieces[1 + direction] + pressure
    sound = jnp.sqrt(1.4 * pressure / density)
    return (jnp.stack(pieces), jnp.abs(speed) + sound)


def common_flux(left_state, right_state, direction):
    left_flux, left_wave = euler_flux(left_state, direction)
    right_flux, right_wave = euler_flux(right_state, direction)
    wave = jnp.maximum(left_wave, right_wave)
    return 0.5 * (left_flux + right_flux) - 0.5 * wave * (right_state - left_state)


def remote_fluxes(left_states, right_states):
    return jnp.stack(
        [
            common_flux(left_states[direction], right_states[direction], direction)
            for direction in range(3)
        ]
    )


def slot_states(state, plus_rows, minus_rows):
    deriv, lower, upper, lift_low, lift_high = tables()
    columns = state.shape[-1]
    grid_form = state.reshape(5, 5, 5, 5, columns)
    high_slots = []
    low_slots = []
    for direction in range(3):
        high_face = jnp.einsum(face_forms[direction], upper, grid_form, precision=precise).reshape(
            5, 25, columns
        )
        low_face = jnp.einsum(face_forms[direction], lower, grid_form, precision=precise).reshape(
            5, 25, columns
        )
        high_slots.append(jnp.take(high_face, plus_rows[direction], axis=2))
        low_slots.append(jnp.take(low_face, minus_rows[direction], axis=2))
    return (jnp.stack(high_slots), jnp.stack(low_slots))


def interpolate(state, cells, weights, blocks):
    block_width = cells.shape[0] // blocks

    def one_block(index):
        block_cells = lax.dynamic_slice_in_dim(cells, index * block_width, block_width)
        block_weights = lax.dynamic_slice_in_dim(weights, index * block_width, block_width, axis=2)
        gathered = jnp.take(state, block_cells, axis=2).reshape(5, 5, 5, 5, block_width)
        reduced = jnp.einsum("as,vabcs->vbcs", block_weights[0], gathered, precision=precise)
        reduced = jnp.einsum("bs,vbcs->vcs", block_weights[1], reduced, precision=precise)
        return jnp.einsum("cs,vcs->vs", block_weights[2], reduced, precision=precise)

    values = lax.map(one_block, jnp.arange(blocks, dtype=jnp.int32))
    return jnp.transpose(values, (1, 0, 2)).reshape(5, blocks * block_width)


def inverse_order(rows):
    count = rows.shape[0]
    return jnp.zeros((count,), jnp.int32).at[rows].set(jnp.arange(count, dtype=jnp.int32))


def assemble(high_slots, low_slots, remote_plus, remote_minus, fringe, plus_rows, minus_rows):
    remote = remote_plus.shape[-1]
    start = remote + fringe.shape[-1]
    plus_parts = []
    minus_parts = []
    for direction in range(3):
        local_flux = common_flux(
            high_slots[direction][:, :, start:], low_slots[direction][:, :, start:], direction
        )
        fringe_high = common_flux(
            high_slots[direction][:, :, remote:start], fringe[direction, 1], direction
        )
        fringe_low = common_flux(
            fringe[direction, 0], low_slots[direction][:, :, remote:start], direction
        )
        plus_slots = jnp.concatenate([remote_plus[direction], fringe_high, local_flux], axis=2)
        minus_slots = jnp.concatenate([remote_minus[direction], fringe_low, local_flux], axis=2)
        plus_parts.append(jnp.take(plus_slots, inverse_order(plus_rows[direction]), axis=2))
        minus_parts.append(jnp.take(minus_slots, inverse_order(minus_rows[direction]), axis=2))
    return (jnp.stack(plus_parts), jnp.stack(minus_parts))


def divergence(state, scales, plus_common, minus_common):
    deriv, lower, upper, lift_low, lift_high = tables()
    columns = state.shape[-1]
    grid_form = state.reshape(5, 5, 5, 5, columns)
    total = jnp.zeros_like(grid_form)
    for direction in range(3):
        flux = euler_flux(grid_form, direction)[0]
        inner = jnp.einsum(volume_forms[direction], deriv, flux, precision=precise)
        low_jump = minus_common[direction].reshape(5, 5, 5, columns) - jnp.einsum(
            face_forms[direction], lower, flux, precision=precise
        )
        high_jump = plus_common[direction].reshape(5, 5, 5, columns) - jnp.einsum(
            face_forms[direction], upper, flux, precision=precise
        )
        inner = inner + jnp.einsum(lift_forms[direction], lift_low, low_jump, precision=precise)
        inner = inner + jnp.einsum(lift_forms[direction], lift_high, high_jump, precision=precise)
        total = total + scales[direction] * inner
    return (-total).reshape(5, 125, columns)


def body(state, inv_size, plus_order, minus_order, donor_cell, donor_weights, recv_slot):
    columns = state.shape[-1]
    part_count = lax.axis_size("dom")
    grid_count = lax.axis_size("grid")
    capacity = max(1, columns // (3 * part_count))
    remote = part_count * capacity
    fringe_count = recv_slot.shape[-1] // 150
    high_slots, low_slots = slot_states(state, plus_order, minus_order)
    values = interpolate(state, donor_cell[0], donor_weights[0], grid_count)
    slot_count = values.shape[1] // (grid_count * part_count)
    shaped = values.reshape(5, grid_count, part_count, slot_count)
    arrived = lax.all_to_all(
        lax.all_to_all(shaped, "grid", split_axis=1, concat_axis=1, tiled=True),
        "dom",
        split_axis=2,
        concat_axis=2,
        tiled=True,
    )
    arrived = arrived.reshape(5, grid_count * part_count * slot_count)
    fringe = jnp.take(arrived, recv_slot[0], axis=1)
    fringe = jnp.transpose(fringe.reshape(5, 3, 2, 25, fringe_count), (1, 2, 0, 3, 4))
    own_high = high_slots[..., :remote]
    own_low = low_slots[..., :remote]
    outgoing = own_low.reshape(3, 5, 25, part_count, capacity)
    partner_low = lax.all_to_all(outgoing, "dom", split_axis=3, concat_axis=3, tiled=True).reshape(
        3, 5, 25, remote
    )
    remote_plus = remote_fluxes(own_high, partner_low)
    returned = lax.all_to_all(
        remote_plus.reshape(3, 5, 25, part_count, capacity),
        "dom",
        split_axis=3,
        concat_axis=3,
        tiled=True,
    )
    remote_minus = returned.reshape(3, 5, 25, remote)
    plus_common, minus_common = assemble(
        high_slots, low_slots, remote_plus, remote_minus, fringe, plus_order, minus_order
    )
    return divergence(state, inv_size, plus_common, minus_common)


def solution(mesh):
    return jax.shard_map(
        body,
        mesh=mesh,
        in_specs=(
            P(None, None, ("grid", "dom")),
            P(None, ("grid", "dom")),
            P(None, ("grid", "dom")),
            P(None, ("grid", "dom")),
            P(("grid", "dom"), None),
            P(("grid", "dom"), None, None, None),
            P(("grid", "dom"), None),
        ),
        out_specs=P(None, None, ("grid", "dom")),
        check_vma=False,
    )
```

profile of v0, /device:TPU:8, one launch (start us, length us, event | category | flops | bytes accessed | tf_op | source)
XLA Modules:
  0.0 255.1 jit_solution(12432255003614025478)
XLA Ops:
  0.0 1.2 copy.2740
  1.3 58.2 %while.10 = (s32[]{:T(128)}, f32[16,5,64]{2,1,0:T(8,128)S(1)}, s32[16]{0:T(128)S(1)}, s32[1024]{0:T(1024)}, f32[5,125,128]{1,0,2:T(8,128)S(1)}, /*index=5*/f32[3...) while((s32[]{:T(128)}, f32[16,5,64]{2,1,0:T(8,128)S(1)}, ...), condition=%wide.region_8.10_spmd, body=%wide.region_7.9_spmd.sunk | while | flops 130696 | bytes 1246307 | solution.py:132
  60.5 9.6 %all-to-all-start.2 = ((f32[16,1,320]{2,1,0:T(1,128)}), f32[16,1,320]{2,1,0:T(1,128)}, u32[]{:S(2)}, u32[]{:S(2)}) async-start(f32[16,1,320]{2,1,0:T(1,128)} %reshape.3685), calls=%async_computation.2 | async-start | bytes 49152 | tf_op jit(solution)/shard_map/all_to_all | solution.py:195
  78.8 1.2 fusion.220
  84.0 1.2 fusion.221
  95.3 1.0 scatter_custom_fusion
  98.5 0.9 fusion.36
  102.5 1.0 scatter_custom_fusion.3
  104.7 1.0 scatter_custom_fusion.2
  106.7 1.2 scatter_custom_fusion.1
  111.9 1.2 fusion.224
  113.1 1.2 fusion.20
  114.3 1.2 fusion.18
  115.5 1.2 fusion.225
  116.7 1.0 copy.2844
  118.3 2.5 gather_fusion.5
  121.4 1.9 fusion.39
  126.7 1.2 scatter_custom_fusion.5
  129.1 1.4 fusion.22
  130.4 1.4 fusion.16
  131.9 1.2 fusion.12
  133.1 1.1 scatter_custom_fusion.4
  135.3 1.2 fusion.14
  160.0 0.9 copy-done.32
  160.9 1.7 fusion.30
  164.5 1.4 reduce.22
  167.1 11.6 %all-to-all-start.3 = ((f32[32,1,160]{2,1,0:T(1,128)}), f32[32,1,160]{2,1,0:T(1,128)}, u32[]{:S(2)}, u32[]{:S(2)}) async-start(f32[32,1,160]{2,1,0:T(1,128)} %reshape.3687), calls=%async_computation.3 | async-start | bytes 65536 | tf_op jit(solution)/shard_map/all_to_all | solution.py:194
  180.3 1.3 reduce.24
  183.5 4.7 %all-to-all-done.3 = f32[32,1,160]{2,1,0:T(1,128)} async-done(((f32[32,1,160]{2,1,0:T(1,128)}), f32[32,1,160]{2,1,0:T(1,128)}, u32[]{:S(2)}, u32[]{:S(2)}) %all-to-all-start.3) | async-done | bytes 20512 | tf_op jit(solution)/shard_map/all_to_all | solution.py:194
  188.2 4.9 %all-to-all-start = ((f32[32,1,375]{2,1,0:T(1,128)}), f32[32,1,375]{2,1,0:T(1,128)}, u32[]{:S(2)}, u32[]{:S(2)}) async-start(f32[32,1,375]{2,1,0:T(1,128)} %reshape.3689), calls=%async_computation | async-start | bytes 98304 | tf_op jit(solution)/shard_map/all_to_all | solution.py:207
  193.1 1.5 reduce.23
  195.4 1.8 copy.2745
  197.2 2.3 gather_fusion.1
  199.4 1.2 copy.2747
  204.1 1.5 reduce.25
  208.6 0.9 copy-done.71
  209.5 0.9 copy-done.65
  210.7 1.3 reduce.26
  212.7 10.0 %all-to-all-start.1 = ((f32[32,1,375]{2,1,0:T(1,128)}), f32[32,1,375]{2,1,0:T(1,128)S(1)}, u32[]{:S(2)}, u32[]{:S(2)}) async-start(f32[32,1,375]{2,1,0:T(1,128)} %reshape.3691), calls=%async_computation.1 | async-start | bytes 98304 | tf_op jit(solution)/shard_map/all_to_all | solution.py:211
  226.1 6.2 %all-to-all-done.1 = f32[32,1,375]{2,1,0:T(1,128)S(1)} async-done(((f32[32,1,375]{2,1,0:T(1,128)}), f32[32,1,375]{2,1,0:T(1,128)S(1)}, u32[]{:S(2)}, u32[]{:S(2)}) %all-to-all-start.1) | async-done | bytes 48032 | tf_op jit(solution)/shard_map/all_to_all | solution.py:211
  234.7 0.9 gather_fusion.8
  236.9 0.9 copy-done.14
  238.0 0.9 gather_fusion.11
  240.4 0.9 gather_fusion.10
  242.8 0.9 gather_fusion.9
  245.9 0.9 copy-done.33
  247.1 0.9 gather_fusion.13
  249.5 0.9 gather_fusion.12
  (841 shorter events, 145.0 us)
Async XLA Ops:
  0.0 1.2 copy-start.92
  59.5 10.6 %copy-start = (f32[5,125,128]{2,1,0:T(8,128)S(1)}, f32[5,125,128]{2,1,0:T(8,128)}, u32[]{:S(2)}) copy-start(f32[5,125,128]{2,1,0:T(8,128)} %param.18) | copy-start | bytes 960004
  60.5 103.5 %all-to-all-start.2 = ((f32[16,1,320]{2,1,0:T(1,128)}), f32[16,1,320]{2,1,0:T(1,128)}, u32[]{:S(2)}, u32[]{:S(2)}) async-start(f32[16,1,320]{2,1,0:T(1,128)} %reshape.3685), calls=%async_computation.2 | async-start | bytes 49152 | tf_op jit(solution)/shard_map/all_to_all | solution.py:195
  92.9 4.6 %copy-start.41 = (f32[1,5,25,128]{3,0,2,1:T(1,128)S(1)}, f32[1,5,25,128]{3,0,2,1:T(1,128)}, u32[]{:S(2)}) copy-start(f32[1,5,25,128]{3,0,2,1:T(1,128)} %fusion.220) | copy-start | bytes 192004
  113.1 1.2 copy-start.103
  115.5 1.2 copy-start.40
  116.7 1.0 copy-start.94
  126.7 2.4 copy-start.93
  135.3 1.2 copy-start.51
  138.5 1.0 copy-start.85
  138.5 1.0 copy-start.84
  138.5 1.9 copy-start.72
  138.5 2.5 copy-start.7
  140.3 17.4 %copy-start.17 = (f32[1,1,25,32]{2,3,1,0:T(8,128)}, f32[1,1,25,32]{2,3,1,0:T(8,128)S(1)}, u32[]{:S(2)}) copy-start(f32[1,1,25,32]{2,3,1,0:T(8,128)S(1)} %copy.2908) | copy-start | bytes 9604
  140.4 17.3 %copy-start.19 = (f32[25,32]{0,1:T(8,128)}, f32[25,32]{0,1:T(8,128)S(1)}, u32[]{:S(2)}) copy-start(f32[25,32]{0,1:T(8,128)S(1)} %copy.2728) | copy-start | bytes 9604
  140.4 1.5 copy-start.6
  141.1 1.6 copy-start.5
  142.7 1.0 copy-start.81
  143.5 1.7 copy-start.69
  144.3 10.4 %copy-start.21 = (f32[1,1,25,32]{2,3,1,0:T(8,128)}, f32[1,1,25,32]{2,3,1,0:T(8,128)S(1)}, u32[]{:S(2)}) copy-start(f32[1,1,25,32]{2,3,1,0:T(8,128)S(1)} %copy.2895) | copy-start | bytes 9604
  144.4 10.3 %copy-start.23 = (f32[25,32]{0,1:T(8,128)}, f32[25,32]{0,1:T(8,128)S(1)}, u32[]{:S(2)}) copy-start(f32[25,32]{0,1:T(8,128)S(1)} %copy.2712) | copy-start | bytes 9604
  145.9 1.7 copy-start.63
  146.0 2.6 %copy-start.25 = (f32[1,1,25,32]{2,3,1,0:T(8,128)}, f32[1,1,25,32]{2,3,1,0:T(8,128)S(1)}, u32[]{:S(2)}) copy-start(f32[1,1,25,32]{2,3,1,0:T(8,128)S(1)} %copy.2882) | copy-start | bytes 9604
  146.2 2.4 copy-start.27
  150.0 1.0 copy-start.61
  151.9 2.0 copy-start.31
  152.5 2.3 copy-start.115
  153.8 0.9 copy-start.57
  153.8 1.6 copy-start.54
  154.7 1.8 copy-start.2
  156.8 2.3 copy-start.30
  159.0 0.9 copy-start.36
  159.0 1.0 copy-start.37
  160.0 0.9 copy-start.32
  160.0 0.9 copy-start.48
  166.2 12.4 %copy-start.126 = (s32[128]{0:T(128)S(1)}, s32[128]{0:T(128)}, u32[]{:S(2)}) copy-start(s32[128]{0:T(128)} %compare_select_fusion.3) | copy-start | bytes 1540
  166.2 12.4 %copy-start.127 = (s32[128]{0:T(128)S(1)}, s32[128]{0:T(128)}, u32[]{:S(2)}) copy-start(s32[128]{0:T(128)} %compare_select_fusion.4) | copy-start | bytes 1540
  166.2 13.0 %copy-start.75 = (pred[3,2,25,4]{3,2,1,0:T(8,128)(4,1)S(1)}, pred[3,2,25,4]{3,2,1,0:T(8,128)(4,1)}, u32[]{:S(2)}) copy-start(pred[3,2,25,4]{3,2,1,0:T(8,128)(4,1)} %compare_and_fusion.1) | copy-start | bytes 1804
  167.1 12.3 %copy-start.9 = (f32[5,25,128]{2,1,0:T(8,128)S(1)}, f32[5,25,128]{2,1,0:T(8,128)}, u32[]{:S(2)}) copy-start(f32[5,25,128]{2,1,0:T(8,128)} %copy-done.8) | copy-start | bytes 192004
  167.1 21.1 %all-to-all-start.3 = ((f32[32,1,160]{2,1,0:T(1,128)}), f32[32,1,160]{2,1,0:T(1,128)}, u32[]{:S(2)}, u32[]{:S(2)}) async-start(f32[32,1,160]{2,1,0:T(1,128)} %reshape.3687), calls=%async_computation.3 | async-start | bytes 65536 | tf_op jit(solution)/shard_map/all_to_all | solution.py:194
  188.2 15.9 %all-to-all-start = ((f32[32,1,375]{2,1,0:T(1,128)}), f32[32,1,375]{2,1,0:T(1,128)}, u32[]{:S(2)}, u32[]{:S(2)}) async-start(f32[32,1,375]{2,1,0:T(1,128)} %reshape.3689), calls=%async_computation | async-start | bytes 98304 | tf_op jit(solution)/shard_map/all_to_all | solution.py:207
  199.4 1.3 copy-start.101
  199.4 1.3 copy-start.98
  212.7 19.6 %all-to-all-start.1 = ((f32[32,1,375]{2,1,0:T(1,128)}), f32[32,1,375]{2,1,0:T(1,128)S(1)}, u32[]{:S(2)}, u32[]{:S(2)}) async-start(f32[32,1,375]{2,1,0:T(1,128)} %reshape.3691), calls=%async_computation.1 | async-start | bytes 98304 | tf_op jit(solution)/shard_map/all_to_all | solution.py:211
  233.4 1.0 copy-start.15
  236.8 0.9 copy-start.14
  250.6 1.1 copy-start.3
  252.3 1.0 copy-start.4
  (84 other events, 64.9 us)
where the time goes:
time: 258 us; the launch traced here: 255 us
  local copies, waits for them, and re-layouts  120 us (47%)
  other arithmetic  60 us (23%)
  starting transfers between devices  36.1 us (14%)
  matrix products  15.5 us (6%)
  waiting for transfers between devices  11 us (4%)
  loops' own time  10.8 us (4%)
    unnamed x296, local copies, waits for them, and re-layouts  47.7 us
    gather x48, local copies, waits for them, and re-layouts, one_block(): jnp.take(state, block_cells, axis=2).reshape(5, 5, 5, 5, block_width)  14.1 us
    and x16, other arithmetic, one_block(): jnp.take(state, block_cells, axis=2).reshape(5, 5, 5, 5, block_width)  12.3 us
    all_to_all x1, starting transfers between devices, body(): lax.all_to_all(lax.all_to_all(shaped, 'grid', split_axis=1, concat_axis=1...  11.6 us
    another operation x1, loops' own time, interpolate(): values = lax.map(one_block, jnp.arange(blocks, dtype=jnp.int32))  10.8 us
    reduce_sum x18, other arithmetic, euler_flux(): jnp.sum(momenta * momenta, axis=0)  10.1 us
    all_to_all x1, starting transfers between devices, body(): lax.all_to_all(remote_plus.reshape(3, 5, 25, part_count, capacity), 'dom'...  9.97 us
    dynamic_slice x16, local copies, waits for them, and re-layouts, interpolate(): values = lax.map(one_block, jnp.arange(blocks, dtype=jnp.int32))  9.94 us
  transfers between devices with their start and end apart: 4, of which 2 were waited for; matrix products, arithmetic and copies ran while one was open for 34% of the time, Pallas kernels for 0%

commit v1 on v0

--- a/solution.py
+++ b/solution.py
@@ -208,12 +208,20 @@
         3, 5, 25, remote
     )
     remote_plus = remote_fluxes(own_high, partner_low)
-    returned = lax.all_to_all(
-        remote_plus.reshape(3, 5, 25, part_count, capacity),
-        "dom",
-        split_axis=3,
-        concat_axis=3,
-        tiled=True,
+    returned = jnp.concatenate(
+        lax.all_to_all(
+            jnp.stack(
+                jnp.split(
+                    remote_plus.reshape(3, 5, 25, part_count, capacity),
+                    lax.axis_size("dom"),
+                    axis=3,
+                )
+            ),
+            "dom",
+            0,
+            0,
+        ),
+        axis=3,
     )
     remote_minus = returned.reshape(3, 5, 25, remote)
     plus_common, minus_common = assemble(

time: 258 us -> 259 us (level)
    unnamed x296 -> x326, local copies, waits for them, and re-layouts: 47.7 us -> 46.9 us
where the time goes in v1:
time: 259 us; the launch traced here: 256 us
  local copies, waits for them, and re-layouts  119 us (46%)
  other arithmetic  60.2 us (23%)
  starting transfers between devices  36.1 us (14%)
  matrix products  15.5 us (6%)
  waiting for transfers between devices  11.5 us (4%)
  loops' own time  11.1 us (4%)
    unnamed x326, local copies, waits for them, and re-layouts  46.9 us
    gather x48, local copies, waits for them, and re-layouts, one_block(): jnp.take(state, block_cells, axis=2).reshape(5, 5, 5, 5, block_width)  14.2 us
    and x16, other arithmetic, one_block(): jnp.take(state, block_cells, axis=2).reshape(5, 5, 5, 5, block_width)  12.3 us
    all_to_all x1, starting transfers between devices, body(): lax.all_to_all(lax.all_to_all(shaped, 'grid', split_axis=1, concat_axis=1...  11.6 us
    another operation x1, loops' own time, interpolate(): values = lax.map(one_block, jnp.arange(blocks, dtype=jnp.int32))  11.1 us
    reduce_sum x18, other arithmetic, euler_flux(): jnp.sum(momenta * momenta, axis=0)  10.2 us
    all_to_all x1, starting transfers between devices, body(): lax.all_to_all(jnp.stack(jnp.split(remote_plus.reshape(3, 5, 25, part_cou...  9.97 us
    dynamic_slice x16, local copies, waits for them, and re-layouts, interpolate(): values = lax.map(one_block, jnp.arange(blocks, dtype=jnp.int32))  9.75 us
  transfers between devices with their start and end apart: 4, of which 2 were waited for; matrix products, arithmetic and copies ran while one was open for 34% of the time, Pallas kernels for 0%

profile of v1, /device:TPU:8, one launch (start us, length us, event | category | flops | bytes accessed | tf_op | source)
XLA Modules:
  0.0 255.6 jit_solution(17516464295910704336)
XLA Ops:
  0.0 1.2 copy.3082
  1.3 58.3 %while.10 = (s32[]{:T(128)}, f32[16,5,64]{2,1,0:T(8,128)S(1)}, s32[16]{0:T(128)S(1)}, s32[1024]{0:T(1024)}, f32[5,125,128]{1,0,2:T(8,128)S(1)}, /*index=5*/f32[3...) while((s32[]{:T(128)}, f32[16,5,64]{2,1,0:T(8,128)S(1)}, ...), condition=%wide.region_8.10_spmd, body=%wide.region_7.9_spmd.sunk | while | flops 130696 | bytes 1246307 | solution.py:132
  60.6 9.6 %all-to-all-start.2 = ((f32[16,1,320]{2,1,0:T(1,128)}), f32[16,1,320]{2,1,0:T(1,128)}, u32[]{:S(2)}, u32[]{:S(2)}) async-start(f32[16,1,320]{2,1,0:T(1,128)} %reshape.3688), calls=%async_computation.2 | async-start | bytes 49152 | tf_op jit(solution)/shard_map/all_to_all | solution.py:195
  79.0 1.2 fusion.219
  84.1 1.2 fusion.220
  95.4 1.0 scatter_custom_fusion
  102.5 1.0 scatter_custom_fusion.3
  104.6 1.0 scatter_custom_fusion.2
  106.8 1.2 scatter_custom_fusion.1
  112.0 1.2 fusion.223
  113.2 1.2 fusion.20
  114.4 1.2 fusion.18
  115.6 1.2 fusion.224
  116.8 1.0 copy.3184
  118.4 2.5 gather_fusion.5
  121.5 1.9 fusion.39
  126.2 1.2 scatter_custom_fusion.5
  128.5 1.4 fusion.22
  129.9 1.4 fusion.16
  131.3 1.2 fusion.12
  132.5 1.1 scatter_custom_fusion.4
  134.7 1.2 fusion.14
  154.0 0.9 copy-done.57
  159.2 1.8 fusion.32
  161.0 0.9 copy-done.33
  164.6 1.5 reduce.22
  167.2 11.6 %all-to-all-start.3 = ((f32[32,1,160]{2,1,0:T(1,128)}), f32[32,1,160]{2,1,0:T(1,128)}, u32[]{:S(2)}, u32[]{:S(2)}) async-start(f32[32,1,160]{2,1,0:T(1,128)} %reshape.3690), calls=%async_computation.3 | async-start | bytes 65536 | tf_op jit(solution)/shard_map/all_to_all | solution.py:194
  180.4 1.3 reduce.24
  183.6 4.7 %all-to-all-done.3 = f32[32,1,160]{2,1,0:T(1,128)} async-done(((f32[32,1,160]{2,1,0:T(1,128)}), f32[32,1,160]{2,1,0:T(1,128)}, u32[]{:S(2)}, u32[]{:S(2)}) %all-to-all-start.3) | async-done | bytes 20512 | tf_op jit(solution)/shard_map/all_to_all | solution.py:194
  188.3 5.0 %all-to-all-start = ((f32[32,1,375]{2,1,0:T(1,128)}), f32[32,1,375]{2,1,0:T(1,128)}, u32[]{:S(2)}, u32[]{:S(2)}) async-start(f32[32,1,375]{2,1,0:T(1,128)} %reshape.3692), calls=%async_computation | async-start | bytes 98304 | tf_op jit(solution)/shard_map/all_to_all | solution.py:207
  193.3 1.5 reduce.23
  195.6 1.7 copy.3087
  197.4 2.3 gather_fusion.1
  199.6 1.2 copy.3089
  204.3 1.6 reduce.25
  208.8 0.9 copy-done.71
  209.7 0.9 copy-done.65
  211.4 1.3 reduce.26
  213.6 10.0 %all-to-all-start.1 = ((f32[32,1,375]{2,1,0:T(1,128)}), f32[32,1,375]{2,1,0:T(1,128)S(1)}, u32[]{:S(2)}, u32[]{:S(2)}) async-start(f32[32,1,375]{2,1,0:T(1,128)} %reshape.3694), calls=%async_computation.1 | async-start | bytes 98304 | tf_op jit(solution)/shard_map/all_to_all | solution.py:212
  224.5 0.9 copy-done.59
  225.4 0.9 copy-done.68
  226.3 6.9 %all-to-all-done.1 = f32[32,1,375]{2,1,0:T(1,128)S(1)} async-done(((f32[32,1,375]{2,1,0:T(1,128)}), f32[32,1,375]{2,1,0:T(1,128)S(1)}, u32[]{:S(2)}, u32[]{:S(2)}) %all-to-all-start.1) | async-done | bytes 48032 | tf_op jit(solution)/shard_map/all_to_all | solution.py:212
  235.7 0.9 gather_fusion.8
  239.2 0.9 gather_fusion.11
  241.6 0.9 gather_fusion.10
  244.0 0.9 gather_fusion.9
  247.4 0.9 gather_fusion.13
  249.8 0.9 gather_fusion.12
  (872 shorter events, 144.3 us)
Async XLA Ops:
  0.0 1.2 copy-start.91
  59.5 10.7 %copy-start = (f32[5,125,128]{2,1,0:T(8,128)S(1)}, f32[5,125,128]{2,1,0:T(8,128)}, u32[]{:S(2)}) copy-start(f32[5,125,128]{2,1,0:T(8,128)} %param.18) | copy-start | bytes 960004
  60.6 103.4 %all-to-all-start.2 = ((f32[16,1,320]{2,1,0:T(1,128)}), f32[16,1,320]{2,1,0:T(1,128)}, u32[]{:S(2)}, u32[]{:S(2)}) async-start(f32[16,1,320]{2,1,0:T(1,128)} %reshape.3688), calls=%async_computation.2 | async-start | bytes 49152 | tf_op jit(solution)/shard_map/all_to_all | solution.py:195
  93.1 4.4 %copy-start.40 = (f32[1,5,25,128]{3,0,2,1:T(1,128)S(1)}, f32[1,5,25,128]{3,0,2,1:T(1,128)}, u32[]{:S(2)}) copy-start(f32[1,5,25,128]{3,0,2,1:T(1,128)} %fusion.219) | copy-start | bytes 192004
  113.2 1.2 copy-start.102
  115.6 1.2 copy-start.39
  116.8 1.0 copy-start.93
  126.2 2.3 copy-start.92
  134.7 1.2 copy-start.51
  137.8 1.9 copy-start.30
  139.8 1.4 copy-start.86
  139.8 1.5 copy-start.85
  139.8 1.6 copy-start.84
  139.8 1.6 copy-start.83
  140.4 2.6 %copy-start.7 = (f32[1,5,25,128]{2,3,1,0:T(8,128)S(1)}, f32[1,5,25,128]{2,3,1,0:T(8,128)}, u32[]{:S(2)}) copy-start(f32[1,5,25,128]{2,3,1,0:T(8,128)} %get-tuple-element.210) | copy-start | bytes 192004
  142.2 15.7 %copy-start.17 = (f32[1,1,25,32]{2,3,1,0:T(8,128)}, f32[1,1,25,32]{2,3,1,0:T(8,128)S(1)}, u32[]{:S(2)}) copy-start(f32[1,1,25,32]{2,3,1,0:T(8,128)S(1)} %copy.3248) | copy-start | bytes 9604
  142.3 15.6 %copy-start.19 = (f32[25,32]{0,1:T(8,128)}, f32[25,32]{0,1:T(8,128)S(1)}, u32[]{:S(2)}) copy-start(f32[25,32]{0,1:T(8,128)S(1)} %copy.3070) | copy-start | bytes 9604
  142.3 1.0 copy-start.6
  143.0 1.1 copy-start.5
  144.1 1.0 copy-start.80
  144.8 1.7 copy-start.69
  145.7 9.1 %copy-start.21 = (f32[1,1,25,32]{2,3,1,0:T(8,128)}, f32[1,1,25,32]{2,3,1,0:T(8,128)S(1)}, u32[]{:S(2)}) copy-start(f32[1,1,25,32]{2,3,1,0:T(8,128)S(1)} %copy.3235) | copy-start | bytes 9604
  145.8 9.1 %copy-start.23 = (f32[25,32]{0,1:T(8,128)}, f32[25,32]{0,1:T(8,128)S(1)}, u32[]{:S(2)}) copy-start(f32[25,32]{0,1:T(8,128)S(1)} %copy.3054) | copy-start | bytes 9604
  147.3 1.7 copy-start.63
  147.4 2.6 %copy-start.25 = (f32[1,1,25,32]{2,3,1,0:T(8,128)}, f32[1,1,25,32]{2,3,1,0:T(8,128)S(1)}, u32[]{:S(2)}) copy-start(f32[1,1,25,32]{2,3,1,0:T(8,128)S(1)} %copy.3222) | copy-start | bytes 9604
  147.6 2.4 copy-start.27
  151.4 1.0 copy-start.61
  153.3 1.6 copy-start.114
  153.9 1.6 copy-start.54
  154.8 1.8 copy-start.2
  156.9 2.2 copy-start.31
  157.9 1.3 copy-start.47
  159.2 1.8 copy-start.35
  159.2 1.8 copy-start.36
  161.0 0.9 copy-start.48
  166.3 12.4 %copy-start.125 = (s32[128]{0:T(128)S(1)}, s32[128]{0:T(128)}, u32[]{:S(2)}) copy-start(s32[128]{0:T(128)} %compare_select_fusion.3) | copy-start | bytes 1540
  166.3 12.4 %copy-start.126 = (s32[128]{0:T(128)S(1)}, s32[128]{0:T(128)}, u32[]{:S(2)}) copy-start(s32[128]{0:T(128)} %compare_select_fusion.4) | copy-start | bytes 1540
  166.4 13.0 %copy-start.74 = (pred[3,2,25,4]{3,2,1,0:T(8,128)(4,1)S(1)}, pred[3,2,25,4]{3,2,1,0:T(8,128)(4,1)}, u32[]{:S(2)}) copy-start(pred[3,2,25,4]{3,2,1,0:T(8,128)(4,1)} %compare_and_fusion.1) | copy-start | bytes 1804
  167.2 12.3 %copy-start.9 = (f32[5,25,128]{2,1,0:T(8,128)S(1)}, f32[5,25,128]{2,1,0:T(8,128)}, u32[]{:S(2)}) copy-start(f32[5,25,128]{2,1,0:T(8,128)} %copy-done.8) | copy-start | bytes 192004
  167.2 21.1 %all-to-all-start.3 = ((f32[32,1,160]{2,1,0:T(1,128)}), f32[32,1,160]{2,1,0:T(1,128)}, u32[]{:S(2)}, u32[]{:S(2)}) async-start(f32[32,1,160]{2,1,0:T(1,128)} %reshape.3690), calls=%async_computation.3 | async-start | bytes 65536 | tf_op jit(solution)/shard_map/all_to_all | solution.py:194
  188.3 16.0 %all-to-all-start = ((f32[32,1,375]{2,1,0:T(1,128)}), f32[32,1,375]{2,1,0:T(1,128)}, u32[]{:S(2)}, u32[]{:S(2)}) async-start(f32[32,1,375]{2,1,0:T(1,128)} %reshape.3692), calls=%async_computation | async-start | bytes 98304 | tf_op jit(solution)/shard_map/all_to_all | solution.py:207
  199.6 1.3 copy-start.100
  199.6 1.3 copy-start.97
  213.6 19.6 %all-to-all-start.1 = ((f32[32,1,375]{2,1,0:T(1,128)}), f32[32,1,375]{2,1,0:T(1,128)S(1)}, u32[]{:S(2)}, u32[]{:S(2)}) async-start(f32[32,1,375]{2,1,0:T(1,128)} %reshape.3694), calls=%async_computation.1 | async-start | bytes 98304 | tf_op jit(solution)/shard_map/all_to_all | solution.py:212
  234.5 1.0 copy-start.15
  237.9 1.0 copy-start.14
  250.9 1.1 copy-start.3
  252.8 1.0 copy-start.4
  (83 other events, 64.5 us)
